TPU v7x, 32 devices: a whole 2x2x4 slice. The times are simulated.
32 devices in a mesh: dp: 8 (over z, y), mp: 4 (over x, core).
Axes of the slice: x: 2, y: 2, z: 4, core: 2. Of those that a mesh axis runs over, the one named last changes fastest.
Arguments:
- tokens: bfloat16 [4096, 2048], P('dp'), may hold values from -6 to 6
- text: bfloat16 [2048, 4096], P('dp', 'mp'), may hold values from -6 to 6
- image_seg: int32 [8, 512], P('dp'), may hold values from 0 to 1, never falling along the last dimension, each value on 1 to 320 neighbouring positions
- text_seg: int32 [8, 256], P('dp'), may hold values from 0 to 1, never falling along the last dimension, each value on 1 to 160 neighbouring positions
- w_qkv: bfloat16 [3, 2048, 2048], P(None, 'dp', 'mp'), may hold values from -0.125 to 0.125
- w_out: bfloat16 [2048, 2048], P('mp', 'dp'), may hold values from -1 to 1
- c_q: bfloat16 [2048, 2048], P('dp', 'mp'), may hold values from -0.125 to 0.125
- c_kv: bfloat16 [2, 4096, 2048], P(None, 'dp', 'mp'), may hold values from -0.09375 to 0.09375
- c_out: bfloat16 [2048, 2048], P('mp', 'dp'), may hold values from -1 to 1
- w_up: bfloat16 [2048, 8192], P('dp', 'mp'), may hold values from -0.125 to 0.125
- w_down: bfloat16 [8192, 2048], P('mp', 'dp'), may hold values from -0.0625 to 0.0625
- norm_gain: float32 [4, 2048], replicated, may hold values from 0.25 to 1.75
- norm_bias: float32 [4, 2048], replicated, may hold values from -4 to 4
- out_bias: float32 [3, 2048], replicated, may hold values from -4 to 4
- up_bias: float32 [8192], P('mp'), may hold values from -4 to 4
- cotangent: bfloat16 [4096, 2048], P('dp'), may hold values from -6 to 6
Outputs:
- output: bfloat16 [4096, 2048], P('dp')
- grad_tokens: float32 [4096, 2048], P('dp')
- grad_text: float32 [2048, 4096], P('dp', 'mp')
- grad_w_qkv: float32 [3, 2048, 2048], P(None, 'dp', 'mp')
- grad_w_out: float32 [2048, 2048], P('mp', 'dp')
- grad_c_q: float32 [2048, 2048], P('dp', 'mp')
- grad_c_kv: float32 [2, 4096, 2048], P(None, 'dp', 'mp')
- grad_c_out: float32 [2048, 2048], P('mp', 'dp')
- grad_w_up: float32 [2048, 8192], P('dp', 'mp')
- grad_w_down: float32 [8192, 2048], P('mp', 'dp')
- grad_norm_gain: float32 [4, 2048], replicated
- grad_norm_bias: float32 [4, 2048], replicated
- grad_out_bias: float32 [3, 2048], replicated
- grad_up_bias: float32 [8192], P('mp')
Inputs may be any that keep to these rules, and one draw needn't show every extreme that they name: In each row image_seg is 0 on the first image and 1 on the second; both images are present, and none has more than 320 tokens. In each row text_seg is 0 on the first caption and 1 on the second; both captions are present, and none has more than 160 tokens.
All inputs are finite; a program needn't handle non-finite values.
Results may differ from a plain program's by a relative error of at most 0.02.
Values may be sent and summed in bfloat16 or wider, within the bound.
No kernel may reach another device: no remote copies, remote signals or barrier semaphores. Data moves between devices by JAX's collectives and lax.ppermute only.
A program may use at most 256 MiB of HBM per device.

v0:
```python
import jax
import jax.numpy as jnp
from jax import lax
from jax.sharding import PartitionSpec as P

HD = 128
eps = 1e-05
masked = -1e30


def normalize(values, gain, shift):
    center = values - jnp.mean(values, axis=-1, keepdims=True)
    spread = jnp.mean(center * center, axis=-1, keepdims=True)
    return center * lax.rsqrt(spread + eps) * gain + shift


def gelu_tanh(values):
    return (
        0.5
        * values
        * (1.0 + jnp.tanh(0.7978845608028654 * (values + 0.044715 * values * values * values)))
    )


def heads_sum(partial_value):
    return lax.psum(partial_value, "mp")


def input_sum(partial_value):
    return lax.psum(partial_value, "mp")


def split_heads(values):
    return values.reshape(values.shape[0], values.shape[1] // HD, HD)


def scores_of(queries, key_rows, allowed):
    raw = jnp.einsum(
        "qhd,khd->hqk",
        split_heads(queries),
        split_heads(key_rows),
        preferred_element_type=jnp.float32,
    ) * HD ** (-0.5)
    return jnp.where(allowed[None], raw, masked)


def attend_forward(queries, key_rows, value_rows, allowed):
    scores = scores_of(queries, key_rows, allowed)
    top = jnp.max(scores, axis=-1, keepdims=True)
    expo = jnp.exp(scores - top)
    total = jnp.sum(expo, axis=-1, keepdims=True)
    probs = (expo / total).astype(jnp.bfloat16)
    mixed = jnp.einsum(
        "hqk,khd->qhd", probs, split_heads(value_rows), preferred_element_type=jnp.float32
    )
    return (
        mixed.reshape(queries.shape[0], queries.shape[1]).astype(jnp.bfloat16),
        top + jnp.log(total),
    )


def attend_backward(queries, key_rows, value_rows, grad_mixed, logsum, allowed):
    scores = scores_of(queries, key_rows, allowed)
    probs = jnp.exp(scores - logsum)
    grad_heads = split_heads(grad_mixed)
    grad_values = jnp.einsum(
        "hqk,qhd->khd", probs.astype(jnp.bfloat16), grad_heads, preferred_element_type=jnp.float32
    )
    grad_probs = jnp.einsum(
        "qhd,khd->hqk", grad_heads, split_heads(value_rows), preferred_element_type=jnp.float32
    )
    grad_scores = (
        probs * (grad_probs - jnp.sum(probs * grad_probs, axis=-1, keepdims=True))
    ).astype(jnp.bfloat16)
    grad_queries = jnp.einsum(
        "hqk,khd->qhd", grad_scores, split_heads(key_rows), preferred_element_type=jnp.float32
    ) * HD ** (-0.5)
    grad_keys = jnp.einsum(
        "hqk,qhd->khd", grad_scores, split_heads(queries), preferred_element_type=jnp.float32
    ) * HD ** (-0.5)
    return (
        grad_queries.reshape(queries.shape),
        grad_keys.reshape(key_rows.shape),
        grad_values.reshape(value_rows.shape),
    )


def on_device(
    tokens,
    text,
    image_seg,
    text_seg,
    w_qkv,
    w_out,
    c_q,
    c_kv,
    c_out,
    w_up,
    w_down,
    norm_gain,
    norm_bias,
    out_bias,
    up_bias,
    cotangent,
):
    row_count = image_seg.shape[0]
    length = image_seg.shape[1]
    text_len = text_seg.shape[1]
    gathered = (
        lax.all_gather(w_qkv, "dp", axis=1, tiled=True),
        lax.all_gather(w_out, "dp", axis=1, tiled=True),
        lax.all_gather(c_q, "dp", axis=0, tiled=True),
        lax.all_gather(c_kv, "dp", axis=1, tiled=True),
        lax.all_gather(c_out, "dp", axis=1, tiled=True),
        lax.all_gather(w_up, "dp", axis=0, tiled=True),
        lax.all_gather(w_down, "dp", axis=1, tiled=True),
    )
    full_qkv, full_out, full_cq, full_ckv, full_cout, full_up, full_down = gathered
    words = lax.all_gather(text, "mp", axis=1, tiled=True)
    same_image = image_seg[:, :, None] == image_seg[:, None, :]
    caption = image_seg[:, :, None] == text_seg[:, None, :]
    residual = tokens.astype(jnp.float32)
    width = full_qkv.shape[2]
    normed_one, pull_one = jax.vjp(normalize, residual, norm_gain[0], norm_bias[0])
    hidden_one = normed_one.astype(jnp.bfloat16)
    projected = jnp.einsum(
        "td,cde->cte", hidden_one, full_qkv, preferred_element_type=jnp.float32
    ).astype(jnp.bfloat16)
    self_inputs = (
        projected[0].reshape(row_count, length, width),
        projected[1].reshape(row_count, length, width),
        projected[2].reshape(row_count, length, width),
    )
    self_mixed, self_logsum = lax.map(
        lambda pieces: attend_forward(*pieces), self_inputs + (same_image,)
    )
    self_flat = self_mixed.reshape(row_count * length, width)
    after_self = (
        residual
        + heads_sum(jnp.dot(self_flat, full_out, preferred_element_type=jnp.float32))
        + out_bias[0]
    )
    normed_two, pull_two = jax.vjp(normalize, after_self, norm_gain[1], norm_bias[1])
    hidden_two = normed_two.astype(jnp.bfloat16)
    cross_query = jnp.dot(hidden_two, full_cq, preferred_element_type=jnp.float32).astype(
        jnp.bfloat16
    )
    text_kv = jnp.einsum("td,cde->cte", words, full_ckv, preferred_element_type=jnp.float32).astype(
        jnp.bfloat16
    )
    cross_inputs = (
        cross_query.reshape(row_count, length, width),
        text_kv[0].reshape(row_count, text_len, width),
        text_kv[1].reshape(row_count, text_len, width),
    )
    cross_mixed, cross_logsum = lax.map(
        lambda pieces: attend_forward(*pieces), cross_inputs + (caption,)
    )
    cross_flat = cross_mixed.reshape(row_count * length, width)
    after_cross = (
        after_self
        + heads_sum(jnp.dot(cross_flat, full_cout, preferred_element_type=jnp.float32))
        + out_bias[1]
    )
    normed_three, pull_three = jax.vjp(normalize, after_cross, norm_gain[2], norm_bias[2])
    hidden_three = normed_three.astype(jnp.bfloat16)
    pre_act = jnp.dot(hidden_three, full_up, preferred_element_type=jnp.float32) + up_bias
    activated, pull_gelu = jax.vjp(gelu_tanh, pre_act)
    act_low = activated.astype(jnp.bfloat16)
    after_mlp = (
        after_cross
        + heads_sum(jnp.dot(act_low, full_down, preferred_element_type=jnp.float32))
        + out_bias[2]
    )
    final, pull_four = jax.vjp(normalize, after_mlp, norm_gain[3], norm_bias[3])
    output = final.astype(jnp.bfloat16)
    grad_mlp, gain_four, shift_four = pull_four(cotangent.astype(jnp.float32))
    grad_mlp_low = grad_mlp.astype(jnp.bfloat16)
    grad_down = jnp.einsum("tf,td->fd", act_low, grad_mlp_low, preferred_element_type=jnp.float32)
    grad_act = jnp.einsum("td,fd->tf", grad_mlp_low, full_down, preferred_element_type=jnp.float32)
    grad_pre = pull_gelu(grad_act)[0].astype(jnp.bfloat16)
    up_bias_grad = jnp.sum(grad_pre.astype(jnp.float32), axis=0)
    grad_up = jnp.einsum("td,tf->df", hidden_three, grad_pre, preferred_element_type=jnp.float32)
    grad_hidden_three = input_sum(
        jnp.einsum("tf,df->td", grad_pre, full_up, preferred_element_type=jnp.float32)
    )
    grad_cross_in, gain_three, shift_three = pull_three(grad_hidden_three)
    grad_after_cross = grad_mlp + grad_cross_in
    grad_cross_low = grad_after_cross.astype(jnp.bfloat16)
    grad_cout = jnp.einsum(
        "te,td->ed", cross_flat, grad_cross_low, preferred_element_type=jnp.float32
    )
    grad_cmix = jnp.einsum(
        "td,ed->te", grad_cross_low, full_cout, preferred_element_type=jnp.float32
    ).astype(jnp.bfloat16)
    cq_grad, ck_grad, cv_grad = lax.map(
        lambda pieces: attend_backward(*pieces),
        cross_inputs + (grad_cmix.reshape(row_count, length, width), cross_logsum, caption),
    )
    cq_low = cq_grad.reshape(row_count * length, width).astype(jnp.bfloat16)
    ckv_low = jnp.stack(
        [ck_grad.reshape(row_count * text_len, width), cv_grad.reshape(row_count * text_len, width)]
    ).astype(jnp.bfloat16)
    grad_cq = jnp.einsum("td,te->de", hidden_two, cq_low, preferred_element_type=jnp.float32)
    grad_ckv = jnp.einsum("td,cte->cde", words, ckv_low, preferred_element_type=jnp.float32)
    text_term = jnp.einsum("cte,cde->td", ckv_low, full_ckv, preferred_element_type=jnp.float32)
    grad_text = lax.psum_scatter(
        text_term.astype(jnp.bfloat16), "mp", scatter_dimension=1, tiled=True
    ).astype(jnp.float32)
    grad_hidden_two = input_sum(
        jnp.einsum("te,de->td", cq_low, full_cq, preferred_element_type=jnp.float32)
    )
    grad_self_in, gain_two, shift_two = pull_two(grad_hidden_two)
    grad_after_self = grad_after_cross + grad_self_in
    grad_self_low = grad_after_self.astype(jnp.bfloat16)
    grad_wout = jnp.einsum(
        "te,td->ed", self_flat, grad_self_low, preferred_element_type=jnp.float32
    )
    grad_smix = jnp.einsum(
        "td,ed->te", grad_self_low, full_out, preferred_element_type=jnp.float32
    ).astype(jnp.bfloat16)
    sq_grad, sk_grad, sv_grad = lax.map(
        lambda pieces: attend_backward(*pieces),
        self_inputs + (grad_smix.reshape(row_count, length, width), self_logsum, same_image),
    )
    qkv_low = jnp.stack(
        [
            sq_grad.reshape(row_count * length, width),
            sk_grad.reshape(row_count * length, width),
            sv_grad.reshape(row_count * length, width),
        ]
    ).astype(jnp.bfloat16)
    grad_qkv = jnp.einsum("td,cte->cde", hidden_one, qkv_low, preferred_element_type=jnp.float32)
    grad_hidden_one = input_sum(
        jnp.einsum("cte,cde->td", qkv_low, full_qkv, preferred_element_type=jnp.float32)
    )
    grad_in_one, gain_one, shift_one = pull_one(grad_hidden_one)
    grad_tokens = grad_after_self + grad_in_one
    gain_terms = jnp.stack([gain_one, gain_two, gain_three, gain_four])
    shift_terms = jnp.stack([shift_one, shift_two, shift_three, shift_four])
    bias_terms = jnp.stack(
        [
            jnp.sum(grad_after_self, axis=0),
            jnp.sum(grad_after_cross, axis=0),
            jnp.sum(grad_mlp, axis=0),
        ]
    )
    gain_total, shift_total, bias_total, up_total = (
        lax.psum(gain_terms.astype(jnp.bfloat16), "dp").astype(jnp.float32),
        lax.psum(shift_terms.astype(jnp.bfloat16), "dp").astype(jnp.float32),
        lax.psum(bias_terms.astype(jnp.bfloat16), "dp").astype(jnp.float32),
        lax.psum(up_bias_grad.astype(jnp.bfloat16), "dp").astype(jnp.float32),
    )
    sum_qkv, sum_wout, sum_cq, sum_ckv, sum_cout, sum_up, sum_down = (
        lax.psum_scatter(
            grad_qkv.astype(jnp.bfloat16), "dp", scatter_dimension=1, tiled=True
        ).astype(jnp.float32),
        lax.psum_scatter(
            grad_wout.astype(jnp.bfloat16), "dp", scatter_dimension=1, tiled=True
        ).astype(jnp.float32),
        lax.psum_scatter(
            grad_cq.astype(jnp.bfloat16), "dp", scatter_dimension=0, tiled=True
        ).astype(jnp.float32),
        lax.psum_scatter(
            grad_ckv.astype(jnp.bfloat16), "dp", scatter_dimension=1, tiled=True
        ).astype(jnp.float32),
        lax.psum_scatter(
            grad_cout.astype(jnp.bfloat16), "dp", scatter_dimension=1, tiled=True
        ).astype(jnp.float32),
        lax.psum_scatter(
            grad_up.astype(jnp.bfloat16), "dp", scatter_dimension=0, tiled=True
        ).astype(jnp.float32),
        lax.psum_scatter(
            grad_down.astype(jnp.bfloat16), "dp", scatter_dimension=1, tiled=True
        ).astype(jnp.float32),
    )
    return (
        output,
        grad_tokens,
        grad_text,
        sum_qkv,
        sum_wout,
        sum_cq,
        sum_ckv,
        sum_cout,
        sum_up,
        sum_down,
        gain_total,
        shift_total,
        bias_total,
        up_total,
    )


def solution(mesh):
    in_specs = (
        P("dp", None),
        P("dp", "mp"),
        P("dp", None),
        P("dp", None),
        P(None, "dp", "mp"),
        P("mp", "dp"),
        P("dp", "mp"),
        P(None, "dp", "mp"),
        P("mp", "dp"),
        P("dp", "mp"),
        P("mp", "dp"),
        P(),
        P(),
        P(),
        P("mp"),
        P("dp", None),
    )
    out_specs = (
        P("dp", None),
        P("dp", None),
        P("dp", "mp"),
        P(None, "dp", "mp"),
        P("mp", "dp"),
        P("dp", "mp"),
        P(None, "dp", "mp"),
        P("mp", "dp"),
        P("dp", "mp"),
        P("mp", "dp"),
        P(),
        P(),
        P(),
        P("mp"),
    )
    return jax.shard_map(
        on_device, mesh=mesh, in_specs=in_specs, out_specs=out_specs, check_vma=False
    )
```

profile of v0, /device:TPU:0, one launch (start us, length us, event | category | flops | bytes accessed | tf_op | source)
XLA Modules:
  0.0 2109.8 jit_solution(6485817762568258638)
XLA Ops:
  13.9 99.0 %all-gather.9.cloned.1.call-done = bf16[3,2048,512]{1,2,0:T(8,128)(2,1)} async-done(((bf16[3,256,512]{1,2,0:T(8,128)(2,1)}), bf16[3,2048,512]{1,2,0:T(8,128)(2,1)}) %all-gather.9.cloned.1.call-update) | async-done | bytes 6291472 | tf_op jit(solution)/shard_map/all_gather | solution.py:110
  124.3 39.2 %all-gather.11.cloned.1.call-done = bf16[512,2048]{1,0:T(8,128)(2,1)} async-done(((bf16[512,256]{1,0:T(8,128)(2,1)}), bf16[512,2048]{1,0:T(8,128)(2,1)}) %all-gather.11.cloned.1.call-update) | async-done | bytes 2097168 | tf_op jit(solution)/shard_map/all_gather | solution.py:111
  172.5 79.7 %all-reduce.8.cloned.1.call-done = f32[512,2048]{1,0:T(8,128)} async-done(((f32[512,2048]{1,0:T(8,128)}), f32[512,2048]{1,0:T(8,128)}) %all-reduce.8.cloned.1.call-update) | async-done | bytes 4194320 | tf_op jit(solution)/shard_map/psum | solution.py:26
  257.8 45.6 %all-gather.17.cloned.1.call-done = bf16[2048,512]{1,0:T(8,128)(2,1)} async-done(((bf16[256,512]{1,0:T(8,128)(2,1)}), bf16[2048,512]{1,0:T(8,128)(2,1)}) %all-gather.17.cloned.1.call-update) | async-done | bytes 2097168 | tf_op jit(solution)/shard_map/all_gather | solution.py:112
  306.4 19.6 all-gather.15.cloned.1.call-done
  326.0 127.4 %all-gather.13.cloned.1.call-done = bf16[2,4096,512]{1,2,0:T(8,128)(2,1)} async-done(((bf16[2,512,512]{1,2,0:T(8,128)(2,1)}), bf16[2,4096,512]{1,2,0:T(8,128)(2,1)}) %all-gather.13.cloned.1.call-update) | async-done | bytes 8388624 | tf_op jit(solution)/shard_map/all_gather | solution.py:113
  461.3 42.8 %all-gather.19.cloned.1.call-done = bf16[512,2048]{1,0:T(8,128)(2,1)} async-done(((bf16[512,256]{1,0:T(8,128)(2,1)}), bf16[512,2048]{1,0:T(8,128)(2,1)}) %all-gather.19.cloned.1.call-update) | async-done | bytes 2097168 | tf_op jit(solution)/shard_map/all_gather | solution.py:114
  510.5 82.3 %all-reduce.10.cloned.1.call-done = f32[512,2048]{1,0:T(8,128)} async-done(((f32[512,2048]{1,0:T(8,128)}), f32[512,2048]{1,0:T(8,128)}) %all-reduce.10.cloned.1.call-update) | async-done | bytes 4194320 | tf_op jit(solution)/shard_map/psum | solution.py:26
  599.3 120.2 %all-gather.21.cloned.1.call-done = bf16[2048,2048]{1,0:T(8,128)(2,1)} async-done(((bf16[256,2048]{1,0:T(8,128)(2,1)}), bf16[2048,2048]{1,0:T(8,128)(2,1)}) %all-gather.21.cloned.1.call-update) | async-done | bytes 8388624 | tf_op jit(solution)/shard_map/all_gather | solution.py:115
  730.7 113.8 %all-gather.23.cloned.1.call-done = bf16[2048,2048]{1,0:T(8,128)(2,1)} async-done(((bf16[2048,256]{1,0:T(8,128)(2,1)}), bf16[2048,2048]{1,0:T(8,128)(2,1)}) %all-gather.23.cloned.1.call-update) | async-done | bytes 8388624 | tf_op jit(solution)/shard_map/all_gather | solution.py:116
  856.4 83.6 %all-reduce.12.cloned.1.call-done = f32[512,2048]{1,0:T(8,128)} async-done(((f32[512,2048]{1,0:T(8,128)}), f32[512,2048]{1,0:T(8,128)}) %all-reduce.12.cloned.1.call-update) | async-done | bytes 4194320 | tf_op jit(solution)/shard_map/psum | solution.py:26
  969.7 85.5 %all-reduce.14.cloned.1.call-done = f32[512,2048]{1,0:T(8,128)} async-done(((f32[512,2048]{1,0:T(8,128)}), f32[512,2048]{1,0:T(8,128)}) %all-reduce.14.cloned.1.call-update) | async-done | bytes 4194320 | tf_op jit(solution)/shard_map/psum | solution.py:30
  1072.5 85.2 %all-reduce.16.cloned.1.call-done = f32[512,2048]{1,0:T(8,128)} async-done(((f32[512,2048]{1,0:T(8,128)}), f32[512,2048]{1,0:T(8,128)}) %all-reduce.16.cloned.1.call-update) | async-done | bytes 4194320 | tf_op jit(solution)/shard_map/psum | solution.py:30
  1218.7 12.4 convolution_convert_fusion
  1260.7 16.9 all-reduce.18.cloned.1.call-done
  1283.1 38.6 %all-reduce = (bf16[4,2048]{1,0:T(4,128)(2,1)S(1)}, bf16[4,2048]{1,0:T(4,128)(2,1)S(1)}, bf16[3,2048]{1,0:T(4,128)(2,1)S(1)}, bf16[2048]{0:T(1024)(128)(2,1)S(1)}) all-reduce(bf16[4,2048]{1,0:T(4,128)(2,1)S(1)} %get-tuple-element.190, bf16[4,2048]{1,0:T(4,128)(2,1)S(1)} %get-tuple-element.191, ...), channel_id=1, replica_groups=mesh['dp'=8,'mp'=4] {'dp'}, use_global_device_ids=true, to_apply=%region_40.41 | all-reduce | flops 24576 | bytes 98304 | tf_op jit(solution)/shard_map/psum | solution.py:249
  1329.8 20.3 reduce-scatter.15.cloned.1.call-done
  1352.0 31.5 %reduce-scatter.9.cloned.1.call-done = bf16[256,1024]{1,0:T(8,128)(2,1)} async-done(((bf16[256,4096]{1,0:T(8,128)(2,1)}), bf16[256,1024]{1,0:T(8,128)(2,1)}) %reduce-scatter.9.cloned.1.call-update) | async-done | bytes 524304 | tf_op jit(solution)/shard_map/reduce_scatter | solution.py:207
  1385.6 70.2 %reduce-scatter.19.cloned.1.call-done = bf16[512,256]{1,0:T(8,128)(2,1)} async-done(((bf16[512,2048]{1,0:T(8,128)(2,1)}), bf16[512,256]{1,0:T(8,128)(2,1)}) %reduce-scatter.19.cloned.1.call-update) | async-done | bytes 262160 | tf_op jit(solution)/shard_map/reduce_scatter | solution.py:267
  1457.5 70.0 %reduce-scatter.13.cloned.1.call-done = bf16[512,256]{1,0:T(8,128)(2,1)} async-done(((bf16[512,2048]{1,0:T(8,128)(2,1)}), bf16[512,256]{1,0:T(8,128)(2,1)}) %reduce-scatter.13.cloned.1.call-update) | async-done | bytes 262160 | tf_op jit(solution)/shard_map/reduce_scatter | solution.py:258
  1529.3 148.7 %reduce-scatter.23.cloned.1.call-done = bf16[2048,256]{1,0:T(8,128)(2,1)} async-done(((bf16[2048,2048]{1,0:T(8,128)(2,1)}), bf16[2048,256]{1,0:T(8,128)(2,1)}) %reduce-scatter.23.cloned.1.call-update) | async-done | bytes 1048592 | tf_op jit(solution)/shard_map/reduce_scatter | solution.py:273
  1680.8 147.4 %reduce-scatter.21.cloned.1.call-done = bf16[256,2048]{1,0:T(8,128)(2,1)} async-done(((bf16[2048,2048]{1,0:T(8,128)(2,1)}), bf16[256,2048]{1,0:T(8,128)(2,1)}) %reduce-scatter.21.cloned.1.call-update) | async-done | bytes 1048592 | tf_op jit(solution)/shard_map/reduce_scatter | solution.py:270
  1830.9 118.5 %reduce-scatter.11.cloned.1.call-done = bf16[3,256,512]{1,2,0:T(8,128)(2,1)} async-done(((bf16[3,2048,512]{1,2,0:T(8,128)(2,1)}), bf16[3,256,512]{1,2,0:T(8,128)(2,1)}) %reduce-scatter.11.cloned.1.call-update) | async-done | bytes 786448 | tf_op jit(solution)/shard_map/reduce_scatter | solution.py:255
  1951.9 148.2 %reduce-scatter.17.cloned.1.call-done = bf16[2,512,512]{1,2,0:T(8,128)(2,1)} async-done(((bf16[2,4096,512]{1,2,0:T(8,128)(2,1)}), bf16[2,512,512]{1,2,0:T(8,128)(2,1)}) %reduce-scatter.17.cloned.1.call-update) | async-done | bytes 1048592 | tf_op jit(solution)/shard_map/reduce_scatter | solution.py:264
  (273 shorter events, 247.6 us)
Async XLA Ops:
  7.2 105.7 %all-gather.9.cloned.1.call-start = ((), (), s32[]{:S(2)}) async-start(), calls=%async_computation.8 | async-start | bytes 7077888 | tf_op jit(solution)/shard_map/all_gather | solution.py:110
  9.7 153.8 %all-gather.11.cloned.1.call-start = ((), (), s32[]{:S(2)}) async-start(), calls=%async_computation.9 | async-start | bytes 2359296 | tf_op jit(solution)/shard_map/all_gather | solution.py:111
  10.5 241.7 %all-reduce.8.cloned.1.call-start = ((), (), s32[]{:S(2)}) async-start(), calls=%async_computation.10 | async-start | bytes 8388608 | tf_op jit(solution)/shard_map/psum | solution.py:26
  168.4 135.1 %all-gather.17.cloned.1.call-start = ((), (), s32[]{:S(2)}) async-start(), calls=%async_computation.13 | async-start | bytes 2359296 | tf_op jit(solution)/shard_map/all_gather | solution.py:112
  169.0 157.0 %all-gather.15.cloned.1.call-start = ((), (), s32[]{:S(2)}) async-start(), calls=%async_computation.12 | async-start | bytes 2621440 | tf_op jit(solution)/shard_map/all_gather | solution.py:119
  169.6 283.9 %all-gather.13.cloned.1.call-start = ((), (), s32[]{:S(2)}) async-start(), calls=%async_computation.11 | async-start | bytes 9437184 | tf_op jit(solution)/shard_map/all_gather | solution.py:113
  171.0 333.1 %all-gather.19.cloned.1.call-start = ((), (), s32[]{:S(2)}) async-start(), calls=%async_computation.14 | async-start | bytes 2359296 | tf_op jit(solution)/shard_map/all_gather | solution.py:114
  171.7 421.0 %all-reduce.10.cloned.1.call-start = ((), (), s32[]{:S(2)}) async-start(), calls=%async_computation.15 | async-start | bytes 8388608 | tf_op jit(solution)/shard_map/psum | solution.py:26
  306.4 153.5 %copy-start.26 = (bf16[512,512]{0,1:T(8,128)(2,1)}, bf16[512,512]{0,1:T(8,128)(2,1)S(1)}, u32[]{:S(2)}) copy-start(bf16[512,512]{0,1:T(8,128)(2,1)S(1)} %convolution_convert_fusion.9) | copy-start | bytes 1572868
  508.9 210.6 %all-gather.21.cloned.1.call-start = ((), (), s32[]{:S(2)}) async-start(), calls=%async_computation.16 | async-start | bytes 9437184 | tf_op jit(solution)/shard_map/all_gather | solution.py:115
  509.7 334.9 %all-gather.23.cloned.1.call-start = ((), (), s32[]{:S(2)}) async-start(), calls=%async_computation.17 | async-start | bytes 9437184 | tf_op jit(solution)/shard_map/all_gather | solution.py:116
  510.2 429.7 %all-reduce.12.cloned.1.call-start = ((), (), s32[]{:S(2)}) async-start(), calls=%async_computation.18 | async-start | bytes 8388608 | tf_op jit(solution)/shard_map/psum | solution.py:26
  719.5 125.0 %copy-start.51 = (f32[2048]{0:T(1024)S(1)}, f32[2048]{0:T(1024)}, u32[]{:S(2)}) copy-start(f32[2048]{0:T(1024)} %param.30) | copy-start | bytes 24580
  856.1 199.1 %all-reduce.14.cloned.1.call-start = ((), (), s32[]{:S(2)}) async-start(), calls=%async_computation.19 | async-start | bytes 8388608 | tf_op jit(solution)/shard_map/psum | solution.py:30
  969.4 188.3 %all-reduce.16.cloned.1.call-start = ((), (), s32[]{:S(2)}) async-start(), calls=%async_computation.20 | async-start | bytes 8388608 | tf_op jit(solution)/shard_map/psum | solution.py:30
  1071.9 205.7 %all-reduce.18.cloned.1.call-start = ((), (), s32[]{:S(2)}) async-start(), calls=%async_computation.21 | async-start | bytes 8388608 | tf_op jit(solution)/shard_map/psum | solution.py:30
  1191.8 158.3 %reduce-scatter.15.cloned.1.call-start = ((), (), s32[]{:S(2)}) async-start(), calls=%async_computation.25 | async-start | bytes 2359296 | tf_op jit(solution)/shard_map/reduce_scatter | solution.py:261
  1196.2 187.2 %reduce-scatter.9.cloned.1.call-start = ((), (), s32[]{:S(2)}) async-start(), calls=%async_computation.22 | async-start | bytes 2621440 | tf_op jit(solution)/shard_map/reduce_scatter | solution.py:207
  1208.7 247.0 %reduce-scatter.19.cloned.1.call-start = ((), (), s32[]{:S(2)}) async-start(), calls=%async_computation.27 | async-start | bytes 2359296 | tf_op jit(solution)/shard_map/reduce_scatter | solution.py:267
  1213.7 313.9 %reduce-scatter.13.cloned.1.call-start = ((), (), s32[]{:S(2)}) async-start(), calls=%async_computation.24 | async-start | bytes 2359296 | tf_op jit(solution)/shard_map/reduce_scatter | solution.py:258
  1218.6 459.5 %reduce-scatter.23.cloned.1.call-start = ((), (), s32[]{:S(2)}) async-start(), calls=%async_computation.29 | async-start | bytes 9437184 | tf_op jit(solution)/shard_map/reduce_scatter | solution.py:273
  1231.1 597.1 %reduce-scatter.21.cloned.1.call-start = ((), (), s32[]{:S(2)}) async-start(), calls=%async_computation.28 | async-start | bytes 9437184 | tf_op jit(solution)/shard_map/reduce_scatter | solution.py:270
  1242.2 707.2 %reduce-scatter.11.cloned.1.call-start = ((), (), s32[]{:S(2)}) async-start(), calls=%async_computation.23 | async-start | bytes 7077888 | tf_op jit(solution)/shard_map/reduce_scatter | solution.py:255
  1251.2 849.0 %reduce-scatter.17.cloned.1.call-start = ((), (), s32[]{:S(2)}) async-start(), calls=%async_computation.26 | async-start | bytes 9437184 | tf_op jit(solution)/shard_map/reduce_scatter | solution.py:264
  (55 other events, 751.6 us)
Sparse Core Ops, SparseCore 0:
  10.6 102.1 all-gather.8
  114.9 48.5 all-gather.10
  168.5 83.6 all-reduce.7
  254.2 49.2 all-gather.16
  304.9 21.0 all-gather.14
  328.5 124.9 all-gather.12
  455.5 48.5 all-gather.18
  509.0 83.6 all-reduce.9
  594.9 124.6 all-gather.20
  721.4 123.1 all-gather.22
  856.2 83.6 all-reduce.11
  969.5 85.6 all-reduce.13
  1072.1 85.6 all-reduce.15
  1191.9 85.6 all-reduce.17
  1281.5 68.5 reduce-scatter.14
  1353.1 30.2 reduce-scatter.8
  1386.8 68.8 reduce-scatter.18
  1459.7 67.8 reduce-scatter.12
  1531.2 146.8 reduce-scatter.22
  1681.6 146.5 reduce-scatter.20
  1831.8 117.5 reduce-scatter.10
  1953.0 147.0 reduce-scatter.16
where the time goes:
time: 2120 us; the launch traced here: 2110 us
  waiting for transfers between devices  1800 us (85%)
  matrix products  151 us (7%)
  other arithmetic  65.1 us (3%)
  blocking collectives  38.6 us (2%)
  local copies, waits for them, and re-layouts  36.8 us (2%)
    psum x3, waiting for transfers between devices, heads_sum(): return lax.psum(partial_value, 'mp')  246 us
    psum x3, waiting for transfers between devices, input_sum(): return lax.psum(partial_value, 'mp')  188 us
    reduce_scatter x1, waiting for transfers between devices, on_device(): lax.psum_scatter(grad_down.astype(jnp.bfloat16), 'dp', scatter_dimension=...  149 us
    reduce_scatter x1, waiting for transfers between devices, on_device(): lax.psum_scatter(grad_ckv.astype(jnp.bfloat16), 'dp', scatter_dimension=1...  148 us
    reduce_scatter x1, waiting for transfers between devices, on_device(): lax.psum_scatter(grad_up.astype(jnp.bfloat16), 'dp', scatter_dimension=0,...  147 us
    all_gather x1, waiting for transfers between devices, on_device(): lax.all_gather(c_kv, 'dp', axis=1, tiled=True)  127 us
    all_gather x1, waiting for transfers between devices, on_device(): lax.all_gather(w_up, 'dp', axis=0, tiled=True)  120 us
    reduce_scatter x1, waiting for transfers between devices, on_device(): lax.psum_scatter(grad_qkv.astype(jnp.bfloat16), 'dp', scatter_dimension=1...  118 us
  transfers between devices with their start and end apart: 22, of which 22 were waited for; matrix products, arithmetic and copies ran while one was open for 7% of the time, Pallas kernels for 0%

commit v1 on v0

--- a/solution.py
+++ b/solution.py
@@ -2,10 +2,17 @@
 import jax.numpy as jnp
 from jax import lax
 from jax.sharding import PartitionSpec as P
+from jax.lax import all_gather
 
 HD = 128
 eps = 1e-05
 masked = -1e30
+
+
+def shelves_use(vector):
+    carry_in = all_gather(vector, "mp")
+    found_now = jnp.sum(carry_in, 0)
+    return found_now
 
 
 def normalize(values, gain, shift):
@@ -27,7 +34,7 @@
 
 
 def input_sum(partial_value):
-    return lax.psum(partial_value, "mp")
+    return shelves_use(partial_value)
 
 
 def split_heads(values):

time: 2120 us -> 2220 us (1.047)
  other arithmetic: 65.1 us -> 116 us
  waiting for transfers between devices: 1800 us -> 1850 us
    all_gather x0 -> x3, waiting for transfers between devices: none -> 262 us  [shelves_use(): carry_in = all_gather(vector, 'mp')]
    psum x3 -> x0, waiting for transfers between devices: 188 us -> none  [input_sum(): return lax.psum(partial_value, 'mp')]
    reduce_scatter x1, waiting for transfers between devices: 149 us -> 91.6 us  [on_device(): lax.psum_scatter(grad_down.astype(jnp.bfloat16), 'dp', scatter_dimension=...]
    reduce_scatter x1, waiting for transfers between devices: 20.3 us -> 61.4 us  [on_device(): lax.psum_scatter(grad_cq.astype(jnp.bfloat16), 'dp', scatter_dimension=0,...]
    reduce_sum x0 -> x3, other arithmetic: none -> 30.5 us  [shelves_use(): found_now = jnp.sum(carry_in, 0)]
  transfers between devices with their start and end apart: 22 -> 22, of which waited for: 22 -> 22; matrix products, arithmetic and copies ran while one was open for 7% -> 8% of each run, Pallas kernels for 0% -> 0%
where the time goes in v1:
time: 2220 us; the launch traced here: 2210 us
  waiting for transfers between devices  1850 us (83%)
  matrix products  156 us (7%)
  other arithmetic  116 us (5%)
  blocking collectives  37.6 us (2%)
  local copies, waits for them, and re-layouts  32.3 us (1%)
    all_gather x3, waiting for transfers between devices, shelves_use(): carry_in = all_gather(vector, 'mp')  262 us
    psum x3, waiting for transfers between devices, heads_sum(): return lax.psum(partial_value, 'mp')  246 us
    reduce_scatter x1, waiting for transfers between devices, on_device(): lax.psum_scatter(grad_ckv.astype(jnp.bfloat16), 'dp', scatter_dimension=1...  149 us
    reduce_scatter x1, waiting for transfers between devices, on_device(): lax.psum_scatter(grad_up.astype(jnp.bfloat16), 'dp', scatter_dimension=0,...  147 us
    all_gather x1, waiting for transfers between devices, on_device(): lax.all_gather(c_kv, 'dp', axis=1, tiled=True)  127 us
    all_gather x1, waiting for transfers between devices, on_device(): lax.all_gather(w_up, 'dp', axis=0, tiled=True)  120 us
    reduce_scatter x1, waiting for transfers between devices, on_device(): lax.psum_scatter(grad_qkv.astype(jnp.bfloat16), 'dp', scatter_dimension=1...  119 us
    all_gather x1, waiting for transfers between devices, on_device(): lax.all_gather(w_down, 'dp', axis=1, tiled=True)  114 us
  transfers between devices with their start and end apart: 22, of which 22 were waited for; matrix products, arithmetic and copies ran while one was open for 8% of the time, Pallas kernels for 0%

profile of v1, /device:TPU:0, one launch (start us, length us, event | category | flops | bytes accessed | tf_op | source)
XLA Modules:
  0.0 2212.6 jit_solution(759549742026464051)
XLA Ops:
  13.5 99.3 %all-gather.15.cloned.1.call-done = bf16[3,2048,512]{1,2,0:T(8,128)(2,1)} async-done(((bf16[3,256,512]{1,2,0:T(8,128)(2,1)}), bf16[3,2048,512]{1,2,0:T(8,128)(2,1)}) %all-gather.15.cloned.1.call-update) | async-done | bytes 6291472 | tf_op jit(solution)/shard_map/all_gather | solution.py:117
  124.4 39.1 %all-gather.17.cloned.1.call-done = bf16[512,2048]{1,0:T(8,128)(2,1)} async-done(((bf16[512,256]{1,0:T(8,128)(2,1)}), bf16[512,2048]{1,0:T(8,128)(2,1)}) %all-gather.17.cloned.1.call-update) | async-done | bytes 2097168 | tf_op jit(solution)/shard_map/all_gather | solution.py:118
  172.1 80.1 %all-reduce.5.cloned.1.call-done = f32[512,2048]{1,0:T(8,128)} async-done(((f32[512,2048]{1,0:T(8,128)}), f32[512,2048]{1,0:T(8,128)}) %all-reduce.5.cloned.1.call-update) | async-done | bytes 4194320 | tf_op jit(solution)/shard_map/psum | solution.py:33
  257.8 45.6 %all-gather.23.cloned.1.call-done = bf16[2048,512]{1,0:T(8,128)(2,1)} async-done(((bf16[256,512]{1,0:T(8,128)(2,1)}), bf16[2048,512]{1,0:T(8,128)(2,1)}) %all-gather.23.cloned.1.call-update) | async-done | bytes 2097168 | tf_op jit(solution)/shard_map/all_gather | solution.py:119
  306.4 19.6 all-gather.21.cloned.1.call-done
  326.0 127.4 %all-gather.19.cloned.1.call-done = bf16[2,4096,512]{1,2,0:T(8,128)(2,1)} async-done(((bf16[2,512,512]{1,2,0:T(8,128)(2,1)}), bf16[2,4096,512]{1,2,0:T(8,128)(2,1)}) %all-gather.19.cloned.1.call-update) | async-done | bytes 8388624 | tf_op jit(solution)/shard_map/all_gather | solution.py:120
  461.3 42.8 %all-gather.25.cloned.1.call-done = bf16[512,2048]{1,0:T(8,128)(2,1)} async-done(((bf16[512,256]{1,0:T(8,128)(2,1)}), bf16[512,2048]{1,0:T(8,128)(2,1)}) %all-gather.25.cloned.1.call-update) | async-done | bytes 2097168 | tf_op jit(solution)/shard_map/all_gather | solution.py:121
  510.5 82.2 %all-reduce.7.cloned.1.call-done = f32[512,2048]{1,0:T(8,128)} async-done(((f32[512,2048]{1,0:T(8,128)}), f32[512,2048]{1,0:T(8,128)}) %all-reduce.7.cloned.1.call-update) | async-done | bytes 4194320 | tf_op jit(solution)/shard_map/psum | solution.py:33
  599.3 120.2 %all-gather.27.cloned.1.call-done = bf16[2048,2048]{1,0:T(8,128)(2,1)} async-done(((bf16[256,2048]{1,0:T(8,128)(2,1)}), bf16[2048,2048]{1,0:T(8,128)(2,1)}) %all-gather.27.cloned.1.call-update) | async-done | bytes 8388624 | tf_op jit(solution)/shard_map/all_gather | solution.py:122
  730.7 113.9 %all-gather.29.cloned.1.call-done = bf16[2048,2048]{1,0:T(8,128)(2,1)} async-done(((bf16[2048,256]{1,0:T(8,128)(2,1)}), bf16[2048,2048]{1,0:T(8,128)(2,1)}) %all-gather.29.cloned.1.call-update) | async-done | bytes 8388624 | tf_op jit(solution)/shard_map/all_gather | solution.py:123
  856.5 83.5 %all-reduce.9.cloned.1.call-done = f32[512,2048]{1,0:T(8,128)} async-done(((f32[512,2048]{1,0:T(8,128)}), f32[512,2048]{1,0:T(8,128)}) %all-reduce.9.cloned.1.call-update) | async-done | bytes 4194320 | tf_op jit(solution)/shard_map/psum | solution.py:33
  970.6 105.7 %all-gather.31.cloned.1.call-done = f32[2048,2048]{1,0:T(8,128)} async-done(((f32[512,2048]{1,0:T(8,128)}), f32[2048,2048]{1,0:T(8,128)}) %all-gather.31.cloned.1.call-update) | async-done | bytes 16777232 | tf_op jit(solution)/shard_map/all_gather | solution.py:13
  1103.4 13.4 convolution_convert_fusion
  1157.5 51.8 %all-gather.33.cloned.1.call-done = f32[2048,2048]{1,0:T(8,128)} async-done(((f32[512,2048]{1,0:T(8,128)}), f32[2048,2048]{1,0:T(8,128)}) %all-gather.33.cloned.1.call-update) | async-done | bytes 16777232 | tf_op jit(solution)/shard_map/all_gather | solution.py:13
  1269.0 91.6 %reduce-scatter.23.cloned.1.call-done = bf16[2048,256]{1,0:T(8,128)(2,1)} async-done(((bf16[2048,2048]{1,0:T(8,128)(2,1)}), bf16[2048,256]{1,0:T(8,128)(2,1)}) %reduce-scatter.23.cloned.1.call-update) | async-done | bytes 1048592 | tf_op jit(solution)/shard_map/reduce_scatter | solution.py:280
  1363.3 147.4 %reduce-scatter.21.cloned.1.call-done = bf16[256,2048]{1,0:T(8,128)(2,1)} async-done(((bf16[2048,2048]{1,0:T(8,128)(2,1)}), bf16[256,2048]{1,0:T(8,128)(2,1)}) %reduce-scatter.21.cloned.1.call-update) | async-done | bytes 1048592 | tf_op jit(solution)/shard_map/reduce_scatter | solution.py:277
  1520.2 61.4 %reduce-scatter.15.cloned.1.call-done = bf16[256,512]{1,0:T(8,128)(2,1)} async-done(((bf16[2048,512]{1,0:T(8,128)(2,1)}), bf16[256,512]{1,0:T(8,128)(2,1)}) %reduce-scatter.15.cloned.1.call-update) | async-done | bytes 262160 | tf_op jit(solution)/shard_map/reduce_scatter | solution.py:268
  1583.3 31.5 %reduce-scatter.9.cloned.1.call-done = bf16[256,1024]{1,0:T(8,128)(2,1)} async-done(((bf16[256,4096]{1,0:T(8,128)(2,1)}), bf16[256,1024]{1,0:T(8,128)(2,1)}) %reduce-scatter.9.cloned.1.call-update) | async-done | bytes 524304 | tf_op jit(solution)/shard_map/reduce_scatter | solution.py:214
  1616.9 70.3 %reduce-scatter.19.cloned.1.call-done = bf16[512,256]{1,0:T(8,128)(2,1)} async-done(((bf16[512,2048]{1,0:T(8,128)(2,1)}), bf16[512,256]{1,0:T(8,128)(2,1)}) %reduce-scatter.19.cloned.1.call-update) | async-done | bytes 262160 | tf_op jit(solution)/shard_map/reduce_scatter | solution.py:274
  1689.0 148.9 %reduce-scatter.17.cloned.1.call-done = bf16[2,512,512]{1,2,0:T(8,128)(2,1)} async-done(((bf16[2,4096,512]{1,2,0:T(8,128)(2,1)}), bf16[2,512,512]{1,2,0:T(8,128)(2,1)}) %reduce-scatter.17.cloned.1.call-update) | async-done | bytes 1048592 | tf_op jit(solution)/shard_map/reduce_scatter | solution.py:271
  1847.3 62.0 %reduce-scatter.13.cloned.1.call-done = bf16[512,256]{1,0:T(8,128)(2,1)} async-done(((bf16[512,2048]{1,0:T(8,128)(2,1)}), bf16[512,256]{1,0:T(8,128)(2,1)}) %reduce-scatter.13.cloned.1.call-update) | async-done | bytes 262160 | tf_op jit(solution)/shard_map/reduce_scatter | solution.py:265
  1911.1 119.4 %reduce-scatter.11.cloned.1.call-done = bf16[3,256,512]{1,2,0:T(8,128)(2,1)} async-done(((bf16[3,2048,512]{1,2,0:T(8,128)(2,1)}), bf16[3,256,512]{1,2,0:T(8,128)(2,1)}) %reduce-scatter.11.cloned.1.call-update) | async-done | bytes 786448 | tf_op jit(solution)/shard_map/reduce_scatter | solution.py:262
  2033.0 104.2 %all-gather.35.cloned.1.call-done = f32[2048,2048]{1,0:T(8,128)} async-done(((f32[512,2048]{1,0:T(8,128)}), f32[2048,2048]{1,0:T(8,128)}) %all-gather.35.cloned.1.call-update) | async-done | bytes 16777232 | tf_op jit(solution)/shard_map/all_gather | solution.py:13
  2165.5 37.6 %all-reduce = (bf16[4,2048]{1,0:T(4,128)(2,1)S(1)}, bf16[4,2048]{1,0:T(4,128)(2,1)S(1)}, bf16[3,2048]{1,0:T(4,128)(2,1)S(1)}, bf16[2048]{0:T(1024)(128)(2,1)S(1)}) all-reduce(bf16[4,2048]{1,0:T(4,128)(2,1)S(1)} %get-tuple-element.186, bf16[4,2048]{1,0:T(4,128)(2,1)S(1)} %get-tuple-element.187, ...), channel_id=1, replica_groups=mesh['dp'=8,'mp'=4] {'dp'}, use_global_device_ids=true, to_apply=%region_40.41 | all-reduce | flops 24576 | bytes 98304 | tf_op jit(solution)/shard_map/psum | solution.py:256
  (313 shorter events, 298.3 us)
Async XLA Ops:
  7.2 105.7 %all-gather.15.cloned.1.call-start = ((), (), s32[]{:S(2)}) async-start(), calls=%async_computation.8 | async-start | bytes 7077888 | tf_op jit(solution)/shard_map/all_gather | solution.py:117
  9.7 153.8 %all-gather.17.cloned.1.call-start = ((), (), s32[]{:S(2)}) async-start(), calls=%async_computation.9 | async-start | bytes 2359296 | tf_op jit(solution)/shard_map/all_gather | solution.py:118
  10.5 241.7 %all-reduce.5.cloned.1.call-start = ((), (), s32[]{:S(2)}) async-start(), calls=%async_computation.10 | async-start | bytes 8388608 | tf_op jit(solution)/shard_map/psum | solution.py:33
  13.5 242.1 %copy-start.43 = (f32[1,2048]{1,0:T(1,128)}, f32[1,2048]{1,0:T(1,128)S(1)}, u32[]{:S(2)}) copy-start(f32[1,2048]{1,0:T(1,128)S(1)} %get-tuple-element.166) | copy-start | bytes 24580
  168.4 135.1 %all-gather.23.cloned.1.call-start = ((), (), s32[]{:S(2)}) async-start(), calls=%async_computation.13 | async-start | bytes 2359296 | tf_op jit(solution)/shard_map/all_gather | solution.py:119
  169.0 157.0 %all-gather.21.cloned.1.call-start = ((), (), s32[]{:S(2)}) async-start(), calls=%async_computation.12 | async-start | bytes 2621440 | tf_op jit(solution)/shard_map/all_gather | solution.py:126
  169.6 283.9 %all-gather.19.cloned.1.call-start = ((), (), s32[]{:S(2)}) async-start(), calls=%async_computation.11 | async-start | bytes 9437184 | tf_op jit(solution)/shard_map/all_gather | solution.py:120
  171.0 333.1 %all-gather.25.cloned.1.call-start = ((), (), s32[]{:S(2)}) async-start(), calls=%async_computation.14 | async-start | bytes 2359296 | tf_op jit(solution)/shard_map/all_gather | solution.py:121
  171.7 421.0 %all-reduce.7.cloned.1.call-start = ((), (), s32[]{:S(2)}) async-start(), calls=%async_computation.15 | async-start | bytes 8388608 | tf_op jit(solution)/shard_map/psum | solution.py:33
  306.4 153.5 %copy-start.28 = (bf16[512,512]{0,1:T(8,128)(2,1)}, bf16[512,512]{0,1:T(8,128)(2,1)S(1)}, u32[]{:S(2)}) copy-start(bf16[512,512]{0,1:T(8,128)(2,1)S(1)} %convolution_convert_fusion.9) | copy-start | bytes 1572868
  508.9 210.6 %all-gather.27.cloned.1.call-start = ((), (), s32[]{:S(2)}) async-start(), calls=%async_computation.16 | async-start | bytes 9437184 | tf_op jit(solution)/shard_map/all_gather | solution.py:122
  509.7 334.9 %all-gather.29.cloned.1.call-start = ((), (), s32[]{:S(2)}) async-start(), calls=%async_computation.17 | async-start | bytes 9437184 | tf_op jit(solution)/shard_map/all_gather | solution.py:123
  510.2 429.7 %all-reduce.9.cloned.1.call-start = ((), (), s32[]{:S(2)}) async-start(), calls=%async_computation.18 | async-start | bytes 8388608 | tf_op jit(solution)/shard_map/psum | solution.py:33
  856.1 220.1 %all-gather.31.cloned.1.call-start = ((), (), s32[]{:S(2)}) async-start(), calls=%async_computation.27 | async-start | bytes 20971520 | tf_op jit(solution)/shard_map/all_gather | solution.py:13
  970.0 239.2 %all-gather.33.cloned.1.call-start = ((), (), s32[]{:S(2)}) async-start(), calls=%async_computation.28 | async-start | bytes 20971520 | tf_op jit(solution)/shard_map/all_gather | solution.py:13
  1103.2 257.4 %reduce-scatter.23.cloned.1.call-start = ((), (), s32[]{:S(2)}) async-start(), calls=%async_computation.26 | async-start | bytes 9437184 | tf_op jit(solution)/shard_map/reduce_scatter | solution.py:280
  1116.8 393.9 %reduce-scatter.21.cloned.1.call-start = ((), (), s32[]{:S(2)}) async-start(), calls=%async_computation.25 | async-start | bytes 9437184 | tf_op jit(solution)/shard_map/reduce_scatter | solution.py:277
  1129.6 451.9 %reduce-scatter.15.cloned.1.call-start = ((), (), s32[]{:S(2)}) async-start(), calls=%async_computation.22 | async-start | bytes 2359296 | tf_op jit(solution)/shard_map/reduce_scatter | solution.py:268
  1134.1 480.7 %reduce-scatter.9.cloned.1.call-start = ((), (), s32[]{:S(2)}) async-start(), calls=%async_computation.19 | async-start | bytes 2621440 | tf_op jit(solution)/shard_map/reduce_scatter | solution.py:214
  1146.7 540.5 %reduce-scatter.19.cloned.1.call-start = ((), (), s32[]{:S(2)}) async-start(), calls=%async_computation.24 | async-start | bytes 2359296 | tf_op jit(solution)/shard_map/reduce_scatter | solution.py:274
  1151.7 686.1 %reduce-scatter.17.cloned.1.call-start = ((), (), s32[]{:S(2)}) async-start(), calls=%async_computation.23 | async-start | bytes 9437184 | tf_op jit(solution)/shard_map/reduce_scatter | solution.py:271
  1157.4 751.9 %reduce-scatter.13.cloned.1.call-start = ((), (), s32[]{:S(2)}) async-start(), calls=%async_computation.21 | async-start | bytes 2359296 | tf_op jit(solution)/shard_map/reduce_scatter | solution.py:265
  1233.2 797.2 %reduce-scatter.11.cloned.1.call-start = ((), (), s32[]{:S(2)}) async-start(), calls=%async_computation.20 | async-start | bytes 7077888 | tf_op jit(solution)/shard_map/reduce_scatter | solution.py:262
  1257.4 879.8 %all-gather.35.cloned.1.call-start = ((), (), s32[]{:S(2)}) async-start(), calls=%async_computation.29 | async-start | bytes 20971520 | tf_op jit(solution)/shard_map/all_gather | solution.py:13
  (72 other events, 1143.7 us)
Sparse Core Ops, SparseCore 0:
  10.6 102.1 all-gather.14
  114.9 48.5 all-gather.16
  168.5 83.6 all-reduce.4
  254.2 49.2 all-gather.22
  304.9 21.0 all-gather.20
  328.5 124.9 all-gather.18
  455.5 48.5 all-gather.24
  509.0 83.6 all-reduce.6
  594.9 124.6 all-gather.26
  721.4 123.1 all-gather.28
  856.3 83.6 all-reduce.8
  970.2 106.0 all-gather.30
  1103.3 105.8 all-gather.32
  1212.7 147.8 reduce-scatter.22
  1364.1 146.5 reduce-scatter.20
  1514.1 67.3 reduce-scatter.14
  1584.5 30.2 reduce-scatter.8
  1618.2 68.9 reduce-scatter.18
  1690.8 146.9 reduce-scatter.16
  1841.2 67.9 reduce-scatter.12
  1912.9 117.4 reduce-scatter.10
  2032.0 105.1 all-gather.34
